TPU v7x, 256 devices: a whole 4x4x8 slice. The times are simulated.
256 devices in a mesh: cube: 8 (over x, core), blk: 32 (over z, y).
Axes of the slice: x: 4, y: 4, z: 8, core: 2. Of those that a mesh axis runs over, the one named last changes fastest.
Arguments:
- right_side: float32 [4, 8, 32, 32, 64], P(None, 'cube', 'blk'), may hold values from -6 to 6
- diag_inverse: float32 [3840, 32768], P('cube', 'blk'), as said below
- panels: float32 [3, 8, 32, 2, 16, 32], P(None, 'cube', 'blk'), may hold values from -1 to 1
- extend_map: int32 [3, 8, 32, 2, 16], P(None, 'cube', 'blk'), may hold values from 0 to 31
Outputs:
- solution: float32 [4, 8, 32, 32, 64], P(None, 'cube', 'blk')
Inputs may be any that keep to these rules, and one draw needn't show every extreme that they name: `extend_map`: each entry names one of the 32 parent rows held by the receiving device. `diag_inverse`: dense real entries.
All inputs are finite; a program needn't handle non-finite values.
Results may differ from a plain program's by a relative error of at most 0.0001.
Values sent between devices are 32-bit elements; how exact they have to be, the bound alone decides.
A program may use at most 64 MiB of HBM per device.

v0:
```python
import jax
import jax.numpy as jnp
from jax import lax
from jax.sharding import PartitionSpec as P


def from_partner(block, axis, apart):
    count = lax.axis_size(axis)
    route = []
    for low in range(count):
        high = low | 1 << apart
        if high != low and high < count:
            route += [(low, high), (high, low)]
    return lax.ppermute(block, axis, route)


def collect_pairs(residual_rows, tree_level, cube_index):
    gathered = residual_rows
    for bit_index in range(tree_level):
        partner_rows = from_partner(gathered, "cube", bit_index)
        lower_side = cube_index // 2**bit_index % 2 == 0
        gathered = jnp.where(
            lower_side,
            jnp.concatenate([gathered, partner_rows], axis=0),
            jnp.concatenate([partner_rows, gathered], axis=0),
        )
    return gathered


def reduce_pairs(partial_value, tree_level, cube_index):
    for bit_index in reversed(range(tree_level)):
        half_rows = partial_value.shape[0] // 2
        lower_rows = partial_value[:half_rows]
        upper_rows = partial_value[half_rows:]
        lower_side = cube_index // 2**bit_index % 2 == 0
        kept_rows = jnp.where(lower_side, lower_rows, upper_rows)
        sent_rows = jnp.where(lower_side, upper_rows, lower_rows)
        partial_value = kept_rows + from_partner(sent_rows, "cube", bit_index)
    return partial_value


def body(right_side, diag_inverse, panels, extend_map):
    highest = lax.Precision.HIGHEST
    levels = right_side.shape[0]
    local_rows = right_side.shape[3]
    columns_k = right_side.shape[4]
    cube_index = lax.axis_index("cube")
    rhs_rows = right_side[:, 0, 0]
    panel_blocks = panels[:, 0, 0]
    row_maps = extend_map[:, 0, 0]
    row_ids = jnp.arange(local_rows, dtype=jnp.int32)
    update = jnp.zeros((local_rows, columns_k), jnp.float32)
    solved = []
    onehots = []
    diag_blocks = []
    for tree_level in range(levels):
        span_rows = 2**tree_level * local_rows
        offset = (2**tree_level - 1) * local_rows
        diag_block = diag_inverse[offset : offset + span_rows]
        diag_blocks.append(diag_block)
        residual_rows = rhs_rows[tree_level] - update
        column = collect_pairs(residual_rows, tree_level, cube_index)

        def term_rows(first_row, row_count, diag_block=diag_block, column=column):
            return jnp.einsum("ir,ik->rk", diag_block, column, precision=highest)

        solved_rows = lax.psum_scatter(
            term_rows(jnp.int32(0), lax.axis_size("blk") * local_rows),
            "blk",
            scatter_dimension=0,
            tiled=True,
        )
        solved.append(solved_rows)
        if tree_level + 1 < levels:
            onehot = (row_maps[tree_level][..., None] == row_ids).astype(jnp.float32)
            onehots.append(onehot)
            upd_rows = jnp.einsum(
                "hmr,rk->hmk", panel_blocks[tree_level], solved_rows, precision=highest
            )
            extended = jnp.einsum("hmt,hmk->htk", onehot, upd_rows, precision=highest)
            update = extended[0] + from_partner(extended[1], "cube", tree_level)
    results = [None] * levels
    parent = None
    for tree_level in reversed(range(levels)):
        span_rows = 2**tree_level * local_rows
        diag_block = diag_blocks[tree_level]
        work_rows = solved[tree_level]
        if parent is not None:
            partner_rows = from_partner(parent, "cube", tree_level)
            parent_pair = jnp.stack([parent, partner_rows], axis=0)
            fetched = jnp.einsum(
                "hmt,htk->hmk", onehots[tree_level], parent_pair, precision=highest
            )
            work_rows = work_rows - jnp.einsum(
                "hmr,hmk->rk", panel_blocks[tree_level], fetched, precision=highest
            )

        def accumulate(running, shard_rows, first_row, diag_block=diag_block):
            return jnp.einsum("ir,rk->ik", diag_block, shard_rows, precision=highest)

        initial = jnp.zeros((span_rows, columns_k), jnp.float32)
        partial_value = accumulate(
            initial, lax.all_gather(work_rows, "blk", axis=0, tiled=True), jnp.int32(0)
        )
        parent = reduce_pairs(partial_value, tree_level, cube_index)
        results[tree_level] = parent
    return jnp.stack(results)[:, None, None]


def solution(mesh):
    placed = (
        P(None, "cube", "blk", None, None),
        P("cube", "blk"),
        P(None, "cube", "blk", None, None, None),
        P(None, "cube", "blk", None, None),
    )
    return jax.shard_map(
        body,
        mesh=mesh,
        in_specs=placed,
        out_specs=P(None, "cube", "blk", None, None),
        check_vma=False,
    )
```

profile of v0, /device:TPU:4, one launch (start us, length us, event | category | flops | bytes accessed | tf_op | source)
XLA Modules:
  0.0 1131.9 jit_solution(12477692200826738122)
XLA Ops:
  6.5 2.9 fusion.15
  9.5 0.7 slice_bitcast_fusion.6
  10.2 216.9 %reduce-scatter.11.cloned.1.call-done = f32[32,64]{1,0:T(8,128)} async-done(((f32[1024,64]{1,0:T(8,128)}), f32[32,64]{1,0:T(8,128)}) %reduce-scatter.11.cloned.1.call-update) | async-done | bytes 8208 | tf_op jit(solution)/shard_map/reduce_scatter | solution.py:67
  227.1 0.9 convolution_bitcast_fusion.12
  228.0 0.3 fusion.59
  228.4 1.2 collective-permute-done
  229.6 0.7 fusion.46
  230.3 0.2 collective-permute-start.1
  230.5 1.0 collective-permute-done.1
  231.5 1.4 convolution_bitcast_fusion.2
  232.8 1.0 copy.16
  233.9 211.4 %reduce-scatter.13.cloned.1.call-done = f32[32,64]{1,0:T(8,128)} async-done(((f32[1024,64]{1,0:T(8,128)}), f32[32,64]{1,0:T(8,128)}) %reduce-scatter.13.cloned.1.call-update) | async-done | bytes 8208
  445.3 0.8 convolution_bitcast_fusion.11
  446.2 0.3 fusion.58
  446.5 1.3 collective-permute-start.2
  447.8 2.5 collective-permute-done.2
  450.4 1.2 collective-permute-done.3
  451.6 1.2 collective-permute-start.4
  452.8 2.7 collective-permute-done.4
  455.5 0.4 convolution_bitcast_fusion
  455.9 1.0 copy.18
  457.0 211.5 %reduce-scatter.15.cloned.1.call-done = f32[32,64]{1,0:T(8,128)} async-done(((f32[1024,64]{1,0:T(8,128)}), f32[32,64]{1,0:T(8,128)}) %reduce-scatter.15.cloned.1.call-update) | async-done | bytes 8208
  668.5 0.8 convolution_bitcast_fusion.10
  669.4 0.3 fusion.57
  669.7 0.6 collective-permute-start.5
  670.3 4.7 collective-permute-done.5
  675.0 1.2 collective-permute-done.6
  676.2 1.2 collective-permute-start.7
  677.4 2.7 collective-permute-done.7
  680.1 0.6 collective-permute-start.8
  680.7 5.2 collective-permute-done.8
  686.0 0.8 convolution_bitcast_fusion.1
  686.8 1.0 copy.20
  687.8 211.4 %reduce-scatter.17.cloned.1.call-done = f32[32,64]{1,0:T(8,128)} async-done(((f32[1024,64]{1,0:T(8,128)}), f32[32,64]{1,0:T(8,128)}) %reduce-scatter.17.cloned.1.call-update) | async-done | bytes 8208 | tf_op jit(solution)/shard_map/reduce_scatter | solution.py:67
  899.2 48.0 %all_gather.12 = f32[1024,64]{1,0:T(8,128)S(1)} all-gather(f32[32,64]{1,0:T(8,128)} %reduce-scatter.17.cloned.1.call-done), channel_id=1, replica_groups=mesh['cube'=8,'blk'=32] {'blk'}, dimensions={0}, use_global_device_ids=true | all-gather | bytes 270336 | tf_op jit(solution)/shard_map/all_gather | solution.py:103
  947.2 1.0 convolution_bitcast_fusion.3
  948.3 0.6 collective-permute-start.9
  948.9 4.9 collective-permute-done.9
  953.9 1.2 collective-permute-start.10
  955.0 2.7 collective-permute-done.10
  958.0 1.2 collective-permute-done.11
  959.3 0.7 collective-permute-start.12
  960.1 4.8 collective-permute-done.12
  964.9 0.2 fusion.22
  965.1 0.3 fusion
  965.4 47.6 %all_gather.13 = f32[1024,64]{1,0:T(8,128)S(1)} all-gather(f32[32,64]{1,0:T(8,128)S(1)} %copy.9), channel_id=1, replica_groups=mesh['cube'=8,'blk'=32] {'blk'}, dimensions={0}, use_global_device_ids=true | all-gather | bytes 270336 | tf_op jit(solution)/shard_map/all_gather | solution.py:103
  1013.1 1.0 convolution_bitcast_fusion.7
  1014.2 1.2 collective-permute-start.13
  1015.4 2.7 collective-permute-done.13
  1018.3 1.2 collective-permute-done.14
  1019.6 1.2 collective-permute-start.15
  1020.9 2.6 collective-permute-done.15
  1023.5 0.2 fusion.26
  1023.7 0.3 fusion.1
  1024.1 48.0 %all_gather.14 = f32[1024,64]{1,0:T(8,128)S(1)} all-gather(f32[32,64]{1,0:T(8,128)S(1)} %copy.10), channel_id=1, replica_groups=mesh['cube'=8,'blk'=32] {'blk'}, dimensions={0}, use_global_device_ids=true | all-gather | bytes 270336 | tf_op jit(solution)/shard_map/all_gather | solution.py:103
  1072.0 1.0 convolution_bitcast_fusion.5
  1073.2 1.2 collective-permute-done.16
  1074.4 0.2 collective-permute-start.17
  1074.6 1.0 collective-permute-done.17
  1075.7 0.2 fusion.30
  1075.9 0.2 fusion.2
  1076.1 47.5 %all_gather.15 = f32[1024,64]{1,0:T(8,128)S(1)} all-gather(f32[32,64]{1,0:T(8,128)S(1)} %fusion.2), channel_id=1, replica_groups=mesh['cube'=8,'blk'=32] {'blk'}, dimensions={0}, use_global_device_ids=true | all-gather | bytes 270336 | tf_op jit(solution)/shard_map/all_gather | solution.py:103
  1123.7 1.0 convolution_bitcast_fusion.4
  1124.7 0.7 copy.13
  (51 shorter events, 1.6 us)
Async XLA Ops:
  6.5 443.8 %copy-start.5 = (f32[4,1,1,32,64]{4,3,2,1,0:T(8,128)S(1)}, f32[4,1,1,32,64]{4,3,2,1,0:T(8,128)}, u32[]{:S(2)}) copy-start(f32[4,1,1,32,64]{4,3,2,1,0:T(8,128)} %param.4) | copy-start | bytes 98308
  6.5 449.0 %copy-start = (f32[480,1024]{1,0:T(8,128)S(1)}, f32[480,1024]{1,0:T(8,128)}, u32[]{:S(2)}) copy-start(f32[480,1024]{1,0:T(8,128)} %param.5) | copy-start | bytes 5898244
  6.5 438.8 %copy-start.1 = (f32[3,1,1,2,16,32]{5,4,3,2,1,0:T(8,128)S(1)}, f32[3,1,1,2,16,32]{5,4,3,2,1,0:T(8,128)}, u32[]{:S(2)}) copy-start(f32[3,1,1,2,16,32]{5,4,3,2,1,0:T(8,128)} %param.6) | copy-start | bytes 36868
  6.5 220.6 %reduce-scatter.11.cloned.1.call-start = ((), (), s32[]{:S(2)}) async-start(), calls=%async_computation.4 | async-start | bytes 540672 | tf_op jit(solution)/shard_map/reduce_scatter | solution.py:67
  9.4 435.9 %reduce-scatter.13.cloned.1.call-start = ((), (), s32[]{:S(2)}) async-start(), calls=%async_computation.5 | async-start | bytes 540672
  228.3 1.3 collective-permute-start
  230.3 1.2 collective-permute-start.1
  233.9 434.6 %reduce-scatter.15.cloned.1.call-start = ((), (), s32[]{:S(2)}) async-start(), calls=%async_computation.6 | async-start | bytes 540672
  446.5 3.8 collective-permute-start.2
  450.3 1.3 collective-permute-start.3
  451.6 3.9 collective-permute-start.4
  457.0 442.3 %reduce-scatter.17.cloned.1.call-start = ((), (), s32[]{:S(2)}) async-start(), calls=%async_computation.7 | async-start | bytes 540672 | tf_op jit(solution)/shard_map/reduce_scatter | solution.py:67
  669.7 5.3 collective-permute-start.5
  675.0 1.2 collective-permute-start.6
  676.2 3.9 collective-permute-start.7
  680.1 5.9 collective-permute-start.8
  686.8 273.2 %copy-start.3 = (f32[32,64]{1,0:T(8,128)S(1)}, f32[32,64]{1,0:T(8,128)}, u32[]{:S(2)}) copy-start(f32[32,64]{1,0:T(8,128)} %reduce-scatter.15.cloned.1.call-done) | copy-start | bytes 24580
  947.2 73.6 %copy-start.2 = (f32[32,64]{1,0:T(8,128)S(1)}, f32[32,64]{1,0:T(8,128)}, u32[]{:S(2)}) copy-start(f32[32,64]{1,0:T(8,128)} %reduce-scatter.13.cloned.1.call-done) | copy-start | bytes 24580
  948.3 5.5 collective-permute-start.9
  953.9 3.9 collective-permute-start.10
  957.9 1.2 collective-permute-start.11
  959.3 5.6 collective-permute-start.12
  965.4 110.5 %copy-start.4 = (f32[32,64]{1,0:T(8,128)S(1)}, f32[32,64]{1,0:T(8,128)}, u32[]{:S(2)}) copy-start(f32[32,64]{1,0:T(8,128)} %reduce-scatter.11.cloned.1.call-done) | copy-start | bytes 24580
  1014.2 3.9 collective-permute-start.13
  1018.3 1.2 collective-permute-start.14
  1019.6 3.9 collective-permute-start.15
  1073.1 1.2 collective-permute-start.16
  1074.4 1.2 collective-permute-start.17
Sparse Core Ops, SparseCore 0:
  11.2 215.9 reduce-scatter.10
  234.0 211.2 reduce-scatter.12
  457.1 211.3 reduce-scatter.14
  687.9 211.2 reduce-scatter.16
where the time goes:
time: 1130 us
  waiting for transfers between devices  896 us (79%)
  blocking collectives  191 us (17%)
  matrix products  14.2 us (1%)
  between operations  13.4 us (1%)
    reduce_scatter x2, waiting for transfers between devices, body(): lax.psum_scatter(term_rows(jnp.int32(0), lax.axis_size('blk') * local_row...  428 us
    unnamed x6, waiting for transfers between devices  423 us
    all_gather x4, blocking collectives, body(): lax.all_gather(work_rows, 'blk', axis=0, tiled=True)  191 us
    ppermute x18, waiting for transfers between devices, from_partner(): return lax.ppermute(block, axis, route)  44.9 us
  transfers between devices with their start and end apart: 22, of which 22 were waited for; matrix products, arithmetic and copies ran while one was open for 0% of the time, Pallas kernels for 0%

commit v1 on v0

--- a/solution.py
+++ b/solution.py
@@ -100,7 +100,11 @@
 
         initial = jnp.zeros((span_rows, columns_k), jnp.float32)
         partial_value = accumulate(
-            initial, lax.all_gather(work_rows, "blk", axis=0, tiled=True), jnp.int32(0)
+            initial,
+            jnp.concatenate(
+                lax.all_to_all(jnp.stack([work_rows] * lax.axis_size("blk")), "blk", 0, 0), axis=0
+            ),
+            jnp.int32(0),
         )
         parent = reduce_pairs(partial_value, tree_level, cube_index)
         results[tree_level] = parent

time: 1130 us -> 1020 us (0.903)
  blocking collectives: 191 us -> 66.6 us
    reduce_scatter x2 -> x4, waiting for transfers between devices: 428 us -> 851 us  [body(): lax.psum_scatter(term_rows(jnp.int32(0), lax.axis_size('blk') * local_row...]
    unnamed x6 -> x4, waiting for transfers between devices: 423 us -> 0.07 us
    all_gather x4 -> x0, blocking collectives: 191 us -> none  [body(): lax.all_gather(work_rows, 'blk', axis=0, tiled=True)]
    all_to_all x0 -> x4, blocking collectives: none -> 66.6 us  [body(): lax.all_to_all(jnp.stack([work_rows] * lax.axis_size('blk')), 'blk', 0, 0)]
where the time goes in v1:
time: 1020 us
  waiting for transfers between devices  896 us (88%)
  blocking collectives  66.6 us (7%)
  matrix products  14.1 us (1%)
  between operations  13.5 us (1%)
  starting transfers between devices  10.8 us (1%)
    reduce_scatter x4, waiting for transfers between devices, body(): lax.psum_scatter(term_rows(jnp.int32(0), lax.axis_size('blk') * local_row...  851 us
    all_to_all x4, blocking collectives, body(): lax.all_to_all(jnp.stack([work_rows] * lax.axis_size('blk')), 'blk', 0, 0)  66.6 us
    ppermute x18, waiting for transfers between devices, from_partner(): return lax.ppermute(block, axis, route)  45 us
  transfers between devices with their start and end apart: 22, of which 22 were waited for; matrix products, arithmetic and copies ran while one was open for 0% of the time, Pallas kernels for 0%

profile of v1, /device:TPU:4, one launch (start us, length us, event | category | flops | bytes accessed | tf_op | source)
XLA Modules:
  0.0 1016.0 jit_solution(13493052934717494582)
XLA Ops:
  6.5 2.9 fusion.15
  9.5 0.7 slice_bitcast_fusion.6
  10.2 216.9 %reduce-scatter.11.cloned.1.call-done = f32[32,64]{1,0:T(8,128)} async-done(((f32[1024,64]{1,0:T(8,128)}), f32[32,64]{1,0:T(8,128)}) %reduce-scatter.11.cloned.1.call-update) | async-done | bytes 8208 | tf_op jit(solution)/shard_map/reduce_scatter | solution.py:67
  227.1 0.9 convolution_bitcast_fusion.12
  228.4 1.2 collective-permute-done
  229.6 0.7 fusion.46
  230.5 1.0 collective-permute-done.1
  231.5 1.4 convolution_bitcast_fusion.2
  232.8 1.0 copy.21
  233.9 211.4 %reduce-scatter.13.cloned.1.call-done = f32[32,64]{1,0:T(8,128)} async-done(((f32[1024,64]{1,0:T(8,128)}), f32[32,64]{1,0:T(8,128)}) %reduce-scatter.13.cloned.1.call-update) | async-done | bytes 8208 | tf_op jit(solution)/shard_map/reduce_scatter | solution.py:67
  445.3 0.8 convolution_bitcast_fusion.11
  446.5 1.3 collective-permute-start.2
  447.7 2.5 collective-permute-done.2
  450.4 1.2 collective-permute-done.3
  451.6 1.2 collective-permute-start.4
  452.8 2.7 collective-permute-done.4
  455.5 0.4 convolution_bitcast_fusion
  455.9 1.0 copy.23
  457.0 211.5 %reduce-scatter.15.cloned.1.call-done = f32[32,64]{1,0:T(8,128)} async-done(((f32[1024,64]{1,0:T(8,128)}), f32[32,64]{1,0:T(8,128)}) %reduce-scatter.15.cloned.1.call-update) | async-done | bytes 8208 | tf_op jit(solution)/shard_map/reduce_scatter | solution.py:67
  668.5 0.8 convolution_bitcast_fusion.10
  669.4 0.3 fusion.57
  669.7 0.7 collective-permute-start.5
  670.3 4.7 collective-permute-done.5
  675.0 1.2 collective-permute-done.6
  676.2 1.2 collective-permute-start.7
  677.4 2.7 collective-permute-done.7
  680.1 0.7 collective-permute-start.8
  680.8 5.2 collective-permute-done.8
  686.0 0.8 convolution_bitcast_fusion.1
  686.8 1.0 copy.25
  687.8 211.5 %reduce-scatter.17.cloned.1.call-done = f32[32,64]{1,0:T(8,128)} async-done(((f32[1024,64]{1,0:T(8,128)}), f32[32,64]{1,0:T(8,128)}) %reduce-scatter.17.cloned.1.call-update) | async-done | bytes 8208 | tf_op jit(solution)/shard_map/reduce_scatter | solution.py:67
  899.3 0.8 stack.30
  900.1 0.3 reshape.59
  900.4 18.2 %all_to_all.20 = f32[32,1,2048]{2,1,0:T(1,128)S(1)} all-to-all(f32[32,1,2048]{2,1,0:T(1,128)S(1)} %reshape.59), channel_id=1, replica_groups=mesh['cube'=8,'blk'=32] {'blk'}, dimensions={0} | all-to-all | bytes 524288 | tf_op jit(solution)/shard_map/all_to_all | solution.py:105
  918.6 0.5 broadcast.14
  919.1 1.3 reduce
  920.6 1.0 convolution_bitcast_fusion.3
  921.7 0.6 collective-permute-start.9
  922.3 4.9 collective-permute-done.9
  927.3 1.4 collective-permute-start.10
  928.6 2.7 collective-permute-done.10
  931.6 1.2 collective-permute-done.11
  932.9 0.6 collective-permute-start.12
  933.4 4.9 collective-permute-done.12
  938.8 0.3 reshape.61
  939.1 16.0 %all_to_all.21 = f32[32,1,2048]{2,1,0:T(1,128)S(1)} all-to-all(f32[32,1,2048]{2,1,0:T(1,128)S(1)} %reshape.61), channel_id=1, replica_groups=mesh['cube'=8,'blk'=32] {'blk'}, dimensions={0} | all-to-all | bytes 524288 | tf_op jit(solution)/shard_map/all_to_all | solution.py:105
  955.2 1.3 reduce.1
  956.6 1.0 convolution_bitcast_fusion.6
  957.7 1.2 collective-permute-start.13
  958.9 2.7 collective-permute-done.13
  961.9 1.2 collective-permute-done.14
  963.1 1.2 collective-permute-start.15
  964.3 2.7 collective-permute-done.15
  967.6 0.3 reshape.63
  967.9 15.8 %all_to_all.22 = f32[32,1,2048]{2,1,0:T(1,128)S(1)} all-to-all(f32[32,1,2048]{2,1,0:T(1,128)S(1)} %reshape.63), channel_id=1, replica_groups=mesh['cube'=8,'blk'=32] {'blk'}, dimensions={0} | all-to-all | bytes 524288 | tf_op jit(solution)/shard_map/all_to_all | solution.py:105
  983.7 1.3 reduce.2
  985.2 1.0 convolution_bitcast_fusion.5
  986.3 1.2 collective-permute-done.16
  987.8 1.0 collective-permute-done.17
  989.3 0.3 reshape.65
  989.6 16.6 %all_to_all.23 = f32[32,1,2048]{2,1,0:T(1,128)S(1)} all-to-all(f32[32,1,2048]{2,1,0:T(1,128)S(1)} %reshape.65), channel_id=1, replica_groups=mesh['cube'=8,'blk'=32] {'blk'}, dimensions={0} | all-to-all | bytes 524288 | tf_op jit(solution)/shard_map/all_to_all | solution.py:105
  1006.3 1.3 reduce.3
  1007.8 1.0 convolution_bitcast_fusion.4
  1008.8 0.7 copy.18
  (64 shorter events, 4.6 us)
Async XLA Ops:
  6.5 449.0 %copy-start = (f32[480,1024]{1,0:T(8,128)S(1)}, f32[480,1024]{1,0:T(8,128)}, u32[]{:S(2)}) copy-start(f32[480,1024]{1,0:T(8,128)} %param.5) | copy-start | bytes 5898244
  6.5 443.7 %copy-start.5 = (f32[4,1,1,32,64]{4,3,2,1,0:T(8,128)S(1)}, f32[4,1,1,32,64]{4,3,2,1,0:T(8,128)}, u32[]{:S(2)}) copy-start(f32[4,1,1,32,64]{4,3,2,1,0:T(8,128)} %param.4) | copy-start | bytes 98308
  6.5 438.8 %copy-start.1 = (f32[3,1,1,2,16,32]{5,4,3,2,1,0:T(8,128)S(1)}, f32[3,1,1,2,16,32]{5,4,3,2,1,0:T(8,128)}, u32[]{:S(2)}) copy-start(f32[3,1,1,2,16,32]{5,4,3,2,1,0:T(8,128)} %param.6) | copy-start | bytes 36868
  6.5 220.6 %reduce-scatter.11.cloned.1.call-start = ((), (), s32[]{:S(2)}) async-start(), calls=%async_computation.8 | async-start | bytes 540672 | tf_op jit(solution)/shard_map/reduce_scatter | solution.py:67
  9.4 435.9 %reduce-scatter.13.cloned.1.call-start = ((), (), s32[]{:S(2)}) async-start(), calls=%async_computation.9 | async-start | bytes 540672 | tf_op jit(solution)/shard_map/reduce_scatter | solution.py:67
  228.3 1.3 collective-permute-start
  230.3 1.2 collective-permute-start.1
  233.9 434.6 %reduce-scatter.15.cloned.1.call-start = ((), (), s32[]{:S(2)}) async-start(), calls=%async_computation.10 | async-start | bytes 540672 | tf_op jit(solution)/shard_map/reduce_scatter | solution.py:67
  446.5 3.8 collective-permute-start.2
  450.3 1.3 collective-permute-start.3
  451.6 3.9 collective-permute-start.4
  457.0 442.4 %reduce-scatter.17.cloned.1.call-start = ((), (), s32[]{:S(2)}) async-start(), calls=%async_computation.11 | async-start | bytes 540672 | tf_op jit(solution)/shard_map/reduce_scatter | solution.py:67
  669.7 5.3 collective-permute-start.5
  675.0 1.2 collective-permute-start.6
  676.2 3.9 collective-permute-start.7
  680.1 5.9 collective-permute-start.8
  918.6 19.9 %copy-start.4 = (f32[32,64]{1,0:T(8,128)S(1)}, f32[32,64]{1,0:T(8,128)}, u32[]{:S(2)}) copy-start(f32[32,64]{1,0:T(8,128)} %reduce-scatter.15.cloned.1.call-done) | copy-start | bytes 24580
  921.7 5.5 collective-permute-start.9
  927.3 4.1 collective-permute-start.10
  931.5 1.2 collective-permute-start.11
  932.9 5.4 collective-permute-start.12
  938.8 28.5 %copy-start.3 = (f32[32,64]{1,0:T(8,128)S(1)}, f32[32,64]{1,0:T(8,128)}, u32[]{:S(2)}) copy-start(f32[32,64]{1,0:T(8,128)} %reduce-scatter.13.cloned.1.call-done) | copy-start | bytes 24580
  957.7 3.9 collective-permute-start.13
  961.8 1.2 collective-permute-start.14
  963.1 3.9 collective-permute-start.15
  967.6 21.4 %copy-start.2 = (f32[32,64]{1,0:T(8,128)S(1)}, f32[32,64]{1,0:T(8,128)}, u32[]{:S(2)}) copy-start(f32[32,64]{1,0:T(8,128)} %reduce-scatter.11.cloned.1.call-done) | copy-start | bytes 24580
  986.2 1.2 collective-permute-start.16
  987.6 1.2 collective-permute-start.17
Sparse Core Ops, SparseCore 0:
  11.2 215.9 reduce-scatter.10
  234.0 211.2 reduce-scatter.12
  457.1 211.3 reduce-scatter.14
  687.9 211.3 reduce-scatter.16
